TPU v7x, 32 devices: a whole 2x2x4 slice. The times are simulated.
32 devices in a mesh: band: 8 (over z, y), head: 4 (over x, core).
Axes of the slice: x: 2, y: 2, z: 4, core: 2. Of those that a mesh axis runs over, the one named last changes fastest.
Arguments:
- grid_feat: bfloat16 [65536, 1024], P(('band', 'head')), may hold values from -7 to 7
- mesh_feat: bfloat16 [4096, 1024], P(('band', 'head')), may hold values from -7 to 7
- enc_query: bfloat16 [1024, 1024], replicated, may hold values from -0.1875 to 0.1875
- enc_keyval: bfloat16 [1024, 2048], replicated, may hold values from -0.1875 to 0.1875
- enc_out: bfloat16 [1024, 1024], replicated, may hold values from -0.1875 to 0.1875
- proc_qkv: bfloat16 [3, 1024, 1024], P(None, None, 'head'), may hold values from -0.1875 to 0.1875
- proc_out: bfloat16 [1024, 1024], P('head'), may hold values from -0.1875 to 0.1875
- tile_ids: int32 [64, 8], P(('band', 'head')), may hold values from 0 to 511, as said below
- key_counts: int32 [64], P(('band', 'head')), may hold values from 128 to 1024, as said below
Outputs:
- mesh_out: bfloat16 [4096, 1024], P(('band', 'head'))
Inputs may be any that keep to these rules, and one draw needn't show every extreme that they name: `tile_ids`: mesh tile m lies on the device that holds mesh rows m * 64; every tile it lists is one of that device's grid tiles (grid rows of the same device) or of the 2 grid tiles just before or just after them. Slots may repeat tiles. `key_counts`: the largest value is reached in every draw.
All inputs are finite; a program needn't handle non-finite values.
Results may differ from a plain program's by a relative error of at most 0.012.
The roundings to bfloat16 on the way count: a program that leaves them out, or rounds other values in their place, can miss the bound.
Values may be sent and summed in bfloat16 or wider, within the bound.
A program may use at most 128 MiB of HBM per device.

v0:
```python
import math
import jax
import jax.numpy as jnp
from jax import lax
from jax.sharding import PartitionSpec as P

D = 1024
HEADS = 16
HALFW = 512
GT = 128
LIST = 8
MT = 64
HALO_TILES = 2


def extended(shard, sides, width):
    for axis, dim in sides:
        size, length = (lax.axis_size(axis), shard.shape[dim])
        up = [(i, (i + 1) % size) for i in range(size - 1)]
        down = [(j, i) for i, j in up]
        last = lax.slice_in_dim(shard, length - width, length, axis=dim)
        first = lax.slice_in_dim(shard, 0, width, axis=dim)
        before = lax.ppermute(last, axis, up)
        after = lax.ppermute(first, axis, down)
        shard = jnp.concatenate([before, shard, after], axis=dim)
    return shard


def masked_softmax(scores, key_mask):
    scores = jnp.where(key_mask, scores, -1e30)
    row_top = jnp.max(scores, axis=-1, keepdims=True)
    weights = jnp.exp(scores - row_top)
    return (weights / jnp.sum(weights, axis=-1, keepdims=True)).astype(jnp.bfloat16)


def local(
    grid_feat, mesh_feat, enc_query, enc_keyval, enc_out, proc_qkv, proc_out, tile_ids, key_counts
):
    grid_count, model_width = grid_feat.shape
    mesh_count = mesh_feat.shape[0]
    tiles_dev = grid_count // GT
    head_size = D // HEADS
    score_scale = head_size ** (-0.5)
    device = lax.axis_index(("band", "head"))
    grid_kv = jnp.dot(grid_feat, enc_keyval, preferred_element_type=jnp.float32).astype(
        jnp.bfloat16
    )
    bordered = extended(
        grid_kv.reshape(tiles_dev, GT * 2 * model_width), ((("band", "head"), 0),), HALO_TILES
    )
    grid_tiles = bordered.reshape(-1, GT, 2 * model_width)
    queries = jnp.dot(mesh_feat, enc_query, preferred_element_type=jnp.float32).astype(jnp.bfloat16)
    local_lists = tile_ids - (device * tiles_dev - HALO_TILES)
    positions = jnp.arange(LIST * GT, dtype=jnp.int32)

    def one_tile(packed):
        query_tile, tile_list, valid = packed
        gathered = grid_tiles[tile_list].reshape(LIST * GT, 2 * model_width)
        key_rows = gathered[:, :model_width].reshape(LIST * GT, HEADS, head_size)
        value_rows = gathered[:, model_width:].reshape(LIST * GT, HEADS, head_size)
        query_heads = query_tile.reshape(MT, HEADS, head_size)
        scores = (
            jnp.einsum("qhd,khd->hqk", query_heads, key_rows, preferred_element_type=jnp.float32)
            * score_scale
        )
        weights = masked_softmax(scores, (positions < valid)[None, None, :])
        attended = jnp.einsum(
            "hqk,khd->qhd", weights, value_rows, preferred_element_type=jnp.float32
        )
        return attended.reshape(MT, model_width).astype(jnp.bfloat16)

    enc_attn = lax.map(
        one_tile, (queries.reshape(mesh_count // MT, MT, model_width), local_lists, key_counts)
    )
    enc_attn = enc_attn.reshape(mesh_count, model_width)
    mesh_state = (
        mesh_feat.astype(jnp.float32)
        + jnp.dot(enc_attn, enc_out, preferred_element_type=jnp.float32)
    ).astype(jnp.bfloat16)
    head_cols = proc_qkv.shape[2]
    piece = lax.all_gather(mesh_state, "head", axis=0, tiled=True)
    product = jnp.einsum("rd,tdc->rtc", piece, proc_qkv, preferred_element_type=jnp.float32)
    projected = product.astype(jnp.bfloat16).reshape(piece.shape[0], 3 * head_cols)
    group_rows = projected.shape[0]
    bordered_kv = extended(projected[:, head_cols:], (("band", 0),), HALFW)
    local_heads = head_cols // head_size
    block_rows = math.gcd(group_rows, 512)
    band_start = lax.axis_index("band") * group_rows
    mesh_total = group_rows * lax.axis_size("band")

    def one_block(block_index):
        first = block_index * block_rows
        span = block_rows + 2 * HALFW
        query_heads = lax.dynamic_slice_in_dim(projected, first, block_rows, 0)[
            :, :head_cols
        ].reshape(block_rows, local_heads, head_size)
        window_rows = lax.dynamic_slice_in_dim(bordered_kv, first, span, 0)
        key_rows = window_rows[:, :head_cols].reshape(span, local_heads, head_size)
        value_rows = window_rows[:, head_cols:].reshape(span, local_heads, head_size)
        query_pos = band_start + first + jnp.arange(block_rows, dtype=jnp.int32)
        key_pos = band_start + first - HALFW + jnp.arange(span, dtype=jnp.int32)
        near = (jnp.abs(query_pos[:, None] - key_pos[None, :]) < HALFW) & (
            (key_pos >= 0) & (key_pos < mesh_total)
        )[None, :]
        scores = (
            jnp.einsum("qhd,khd->hqk", query_heads, key_rows, preferred_element_type=jnp.float32)
            * score_scale
        )
        weights = masked_softmax(scores, near[None, :, :])
        attended = jnp.einsum(
            "hqk,khd->qhd", weights, value_rows, preferred_element_type=jnp.float32
        )
        return attended.reshape(block_rows, head_cols).astype(jnp.bfloat16)

    proc_attn = lax.map(one_block, jnp.arange(group_rows // block_rows, dtype=jnp.int32)).reshape(
        group_rows, head_cols
    )
    own_rows = lax.all_to_all(proc_attn, "head", split_axis=0, concat_axis=1, tiled=True)
    out_weights = lax.all_gather(proc_out, "head", axis=0, tiled=True)
    head_total = jnp.dot(own_rows, out_weights, preferred_element_type=jnp.float32)
    return (mesh_state.astype(jnp.float32) + head_total).astype(jnp.bfloat16)


def solution(mesh):
    return jax.shard_map(
        local,
        mesh=mesh,
        in_specs=(
            P(("band", "head"), None),
            P(("band", "head"), None),
            P(),
            P(),
            P(),
            P(None, None, "head"),
            P("head", None),
            P(("band", "head"), None),
            P(("band", "head")),
        ),
        out_specs=P(("band", "head"), None),
        check_vma=False,
    )
```

profile of v0, /device:TPU:8, one launch (start us, length us, event | category | flops | bytes accessed | tf_op | source)
XLA Modules:
  0.0 208.6 jit_solution(7345442903268691120)
XLA Ops:
  6.5 12.1 %convolution_convert_fusion = bf16[2048,2048]{1,0:T(8,128)(2,1)S(1)} fusion(bf16[2048,1024]{1,0:T(8,128)(2,1)} %param.11, bf16[1024,2048]{1,0:T(8,128)(2,1)} %param.14), kind=kOutput, calls=%fused_computation.30 | convolution fusion | flops 8594128896 | bytes 16777216 | tf_op jit(solution)/shard_map/dot_general | solution.py:45
  18.6 3.3 %copy-done.3 = bf16[2048,2048]{1,0:T(8,128)(2,1)} copy-done((bf16[2048,2048]{1,0:T(8,128)(2,1)}, bf16[2048,2048]{1,0:T(8,128)(2,1)S(1)}, u32[]{:S(2)}) %copy-start.3) | copy-done | bytes 8388632
  23.1 3.0 %slice.36 = bf16[2,262144]{1,0:T(2,128)(2,1)} reshape(bf16[256,2048]{1,0:T(8,128)(2,1)} %get-tuple-element.89) | data formatting | bytes 2097152 | tf_op jit(solution)/shard_map/slice | solution.py:22
  26.1 3.7 %collective-permute-start.1 = (bf16[2,262144]{1,0:T(2,128)(2,1)}, bf16[2,262144]{1,0:T(2,128)(2,1)}, u32[]{:S(2)}, u32[]{:S(2)}) collective-permute-start(bf16[2,262144]{1,0:T(2,128)(2,1)} %slice.36), channel_id=1, source_target_pairs={{1,0},{2,1},{3,2},{4,3},{5,4},{6,5},{7,6},{8,7},{9,8},{10,9},{11,1... | collective-permute-start | bytes 3145736 | tf_op jit(solution)/shard_map/ppermute | solution.py:24
  31.5 2.1 %collective-permute-start = (bf16[2,262144]{1,0:T(2,128)(2,1)}, bf16[2,262144]{1,0:T(2,128)(2,1)}, u32[]{:S(2)}, u32[]{:S(2)}) collective-permute-start(bf16[2,262144]{1,0:T(2,128)(2,1)} %slice.34), channel_id=1, source_target_pairs={{0,1},{1,2},{2,3},{3,4},{4,5},{5,6},{6,7},{7,8},{8,9},{9,10},{10,1... | collective-permute-start | bytes 3145736 | tf_op jit(solution)/shard_map/ppermute | solution.py:23
  34.1 8.3 %collective-permute-done.1 = bf16[2,262144]{1,0:T(2,128)(2,1)} collective-permute-done((bf16[2,262144]{1,0:T(2,128)(2,1)}, bf16[2,262144]{1,0:T(2,128)(2,1)}, u32[]{:S(2)}, u32[]{:S(2)}) %collective-permute-start.1) | collective-permute-done | bytes 1048608 | tf_op jit(solution)/shard_map/ppermute | solution.py:24
  44.0 5.8 %collective-permute-done = bf16[2,262144]{1,0:T(2,128)(2,1)} collective-permute-done((bf16[2,262144]{1,0:T(2,128)(2,1)}, bf16[2,262144]{1,0:T(2,128)(2,1)}, u32[]{:S(2)}, u32[]{:S(2)}) %collective-permute-start) | collective-permute-done | bytes 1048608 | tf_op jit(solution)/shard_map/ppermute | solution.py:23
  51.4 10.7 %pad_maximum_fusion = bf16[20,128,2048]{2,1,0:T(8,128)(2,1)} fusion(bf16[2,128,2048]{2,1,0:T(8,128)(2,1)S(1)} %bitcast.79, bf16[16,128,2048]{2,1,0:T(8,128)(2,1)} %bitcast.77, bf16[2,128,2048]{2,1,0:T(8,128)(2,1)S(1)} %bitcast.80), kind=kLoop, calls=%fused_computation.28 | loop fusion | flops 10485760 | bytes 20971520 | tf_op jit(solution)/shard_map/concatenate | solution.py:25
  62.1 52.4 %while.3 = (s32[]{:T(128)}, bf16[2,64,1024]{2,1,0:T(8,128)(2,1)S(1)}, s32[2,8]{1,0:T(2,128)S(1)}, bf16[20,128,2048]{2,1,0:T(8,128)(2,1)}, s32[2]{0:T(128)S(1)}, /*index=5*/bf16[2,64,1024]{2,1,0:T(8,128)(2,1)S(1)}, s32[]{:T(128)}) while((s32[]{:T(128)}, bf16[2,64,1024]{2,1,0:T(8,128)(2,1)S(1)}, s32[2,8]{1,0:T(2,128)S(1)}, ...), condition=%wide.region_3.4_spmd.clone, body=%wide.region_0.3_spmd.clone.sunk | while | flops 276892704 | bytes 55851268 | solution.py:72
  62.2 6.8 %gather_fusion = bf16[8,128,2048]{2,1,0:T(8,128)(2,1)} fusion(bf16[20,128,2048]{2,1,0:T(8,128)(2,1)} %get-tuple-element.156, s32[1024]{0:T(1024)S(1)} %pad_clamp_fusion.2), kind=kCustom, calls=%fused_computation.clone.clone.1 | custom fusion | bytes 8388640 | tf_op jit(solution)/shard_map/while/body/eval_jaxpr/gather | solution.py:58
  69.0 4.6 %fusion.64 = (bf16[1024,1024]{1,0:T(8,128)(2,1)}, bf16[1024,1024]{1,0:T(8,128)(2,1)}) fusion(bf16[1024,2048]{1,0:T(8,128)(2,1)} %bitcast.74), kind=kLoop, calls=%fused_computation.56.clone.1 | loop fusion | bytes 8388608 | tf_op jit(solution)/shard_map/while/body/eval_jaxpr/slice | solution.py:59
  73.6 2.9 %copy.38 = bf16[1024,1024]{0,1:T(8,128)(2,1)S(1)} copy(bf16[1024,1024]{1,0:T(8,128)(2,1)} %get-tuple-element.136) | data formatting | bytes 4194304 | tf_op jit(solution)/shard_map/while
  78.7 3.3 %fusion.66 = (f32[16,64]{1,0:T(8,128)S(1)}, f32[16,64,1024]{2,1,0:T(8,128)}) fusion(f32[16,64,1024]{2,1,0:T(8,128)S(1)} %fusion.65, pred[1024]{0:T(1024)(128)(4,1)S(1)} %iota_compare_fusion.2), kind=kOutput, calls=%fused_computation.57.clone.1 | output fusion | flops 6292479 | bytes 8393728 | tf_op jit(solution)/shard_map/while/body/eval_jaxpr/sub | solution.py:32
  82.0 2.6 %copy.37 = bf16[1024,1024]{0,1:T(8,128)(2,1)} copy(bf16[1024,1024]{1,0:T(8,128)(2,1)S(1)} %copy-done.2) | data formatting | bytes 4194304 | tf_op jit(solution)/shard_map/while
  84.6 3.6 %fusion.67 = bf16[16,64,64]{2,1,0:T(8,128)(2,1)S(1)} fusion(bf16[1024,16,64]{0,2,1:T(8,128)(2,1)} %bitcast.76, f32[16,64,1024]{2,1,0:T(8,128)} %get-tuple-element.137, f32[16,64]{1,0:T(8,128)S(1)} %get-tuple-element.138), kind=kOutput, calls=%fused_computation.11.clone.1 | convolution fusion | flops 136380416 | bytes 6426624 | tf_op jit(solution)/shard_map/while/body/eval_jaxpr/hqk,khd->qhd/dot_general | solution.py:67
  88.4 6.8 %gather_fusion = bf16[8,128,2048]{2,1,0:T(8,128)(2,1)} fusion(bf16[20,128,2048]{2,1,0:T(8,128)(2,1)} %get-tuple-element.156, s32[1024]{0:T(1024)S(1)} %pad_clamp_fusion.2), kind=kCustom, calls=%fused_computation.clone.clone.1 | custom fusion | bytes 8388640 | tf_op jit(solution)/shard_map/while/body/eval_jaxpr/gather | solution.py:58
  95.2 4.6 %fusion.64 = (bf16[1024,1024]{1,0:T(8,128)(2,1)}, bf16[1024,1024]{1,0:T(8,128)(2,1)}) fusion(bf16[1024,2048]{1,0:T(8,128)(2,1)} %bitcast.74), kind=kLoop, calls=%fused_computation.56.clone.1 | loop fusion | bytes 8388608 | tf_op jit(solution)/shard_map/while/body/eval_jaxpr/slice | solution.py:59
  99.8 2.9 %copy.38 = bf16[1024,1024]{0,1:T(8,128)(2,1)S(1)} copy(bf16[1024,1024]{1,0:T(8,128)(2,1)} %get-tuple-element.136) | data formatting | bytes 4194304 | tf_op jit(solution)/shard_map/while
  104.9 3.3 %fusion.66 = (f32[16,64]{1,0:T(8,128)S(1)}, f32[16,64,1024]{2,1,0:T(8,128)}) fusion(f32[16,64,1024]{2,1,0:T(8,128)S(1)} %fusion.65, pred[1024]{0:T(1024)(128)(4,1)S(1)} %iota_compare_fusion.2), kind=kOutput, calls=%fused_computation.57.clone.1 | output fusion | flops 6292479 | bytes 8393728 | tf_op jit(solution)/shard_map/while/body/eval_jaxpr/sub | solution.py:32
  108.2 2.6 %copy.37 = bf16[1024,1024]{0,1:T(8,128)(2,1)} copy(bf16[1024,1024]{1,0:T(8,128)(2,1)S(1)} %copy-done.2) | data formatting | bytes 4194304 | tf_op jit(solution)/shard_map/while
  110.8 3.6 %fusion.67 = bf16[16,64,64]{2,1,0:T(8,128)(2,1)S(1)} fusion(bf16[1024,16,64]{0,2,1:T(8,128)(2,1)} %bitcast.76, f32[16,64,1024]{2,1,0:T(8,128)} %get-tuple-element.137, f32[16,64]{1,0:T(8,128)S(1)} %get-tuple-element.138), kind=kOutput, calls=%fused_computation.11.clone.1 | convolution fusion | flops 136380416 | bytes 6426624 | tf_op jit(solution)/shard_map/while/body/eval_jaxpr/hqk,khd->qhd/dot_general | solution.py:67
  114.5 2.7 %fusion.23 = bf16[128,1024]{1,0:T(8,128)(2,1)} fusion(bf16[128,1024]{1,0:T(8,128)(2,1)S(1)} %bitcast.88, bf16[1024,1024]{1,0:T(8,128)(2,1)} %param.15, bf16[128,1024]{1,0:T(8,128)(2,1)S(1)} %copy-done.5), kind=kOutput, calls=%fused_computation.43 | convolution fusion | flops 268828672 | bytes 2883584 | tf_op jit(solution)/shard_map/dot_general | solution.py:78
  118.1 21.6 %all-gather.3.cloned.1.call-done = bf16[512,1024]{1,0:T(8,128)(2,1)} async-done(((bf16[128,1024]{1,0:T(8,128)(2,1)}), bf16[512,1024]{1,0:T(8,128)(2,1)}) %all-gather.3.cloned.1.call-update) | async-done | bytes 1048592 | tf_op jit(solution)/shard_map/all_gather | solution.py:81
  139.7 2.8 %convolution_convert_fusion.1 = bf16[512,3,256]{0,2,1:T(8,128)(2,1)S(1)} fusion(bf16[3,1024,256]{2,1,0:T(8,128)(2,1)} %param.16, bf16[512,1024]{1,0:T(8,128)(2,1)} %all-gather.3.cloned.1.call-done), kind=kOutput, calls=%fused_computation.38 | convolution fusion | flops 805699584 | bytes 3407872 | tf_op jit(solution)/shard_map/rd,tdc->rtc/dot_general | solution.py:82
  142.5 3.4 %collective-permute-start.2 = (bf16[512,512]{0,1:T(8,128)(2,1)S(1)}, bf16[512,512]{0,1:T(8,128)(2,1)S(1)}, u32[]{:S(2)}, u32[]{:S(2)}) collective-permute-start(bf16[512,512]{0,1:T(8,128)(2,1)S(1)} %slice.49), channel_id=1, source_target_pairs={{0,4},{4,8},{8,12},{12,16},{16,20},{20,24},{24,28},{1,5},{5,9},{9,... | collective-permute-start | bytes 1572872 | tf_op jit(solution)/shard_map/ppermute | solution.py:23
  145.9 3.6 %collective-permute-start.3 = (bf16[512,512]{0,1:T(8,128)(2,1)S(1)}, bf16[512,512]{0,1:T(8,128)(2,1)S(1)}, u32[]{:S(2)}, u32[]{:S(2)}) collective-permute-start(bf16[512,512]{0,1:T(8,128)(2,1)S(1)} %slice.49), channel_id=1, source_target_pairs={{4,0},{8,4},{12,8},{16,12},{20,16},{24,20},{28,24},{5,1},{9,5},{13... | collective-permute-start | bytes 1572872 | tf_op jit(solution)/shard_map/ppermute | solution.py:24
  150.5 18.2 %collective-permute-done.2 = bf16[512,512]{0,1:T(8,128)(2,1)S(1)} collective-permute-done((bf16[512,512]{0,1:T(8,128)(2,1)S(1)}, bf16[512,512]{0,1:T(8,128)(2,1)S(1)}, u32[]{:S(2)}, u32[]{:S(2)}) %collective-permute-start.2) | collective-permute-done | bytes 524320 | tf_op jit(solution)/shard_map/ppermute | solution.py:23
  171.9 9.8 %fusion.35 = (f32[4,512]{1,0:T(4,128)S(1)}, f32[4,512,1536]{2,1,0:T(8,128)}) fusion(pred[512,1536]{1,0:T(8,128)(4,1)S(1)} %fusion.21, bf16[512,4,64]{0,2,1:T(8,128)(2,1)S(1)} %bitcast.87, bf16[1536,4,64]{0,2,1:T(8,128)(2,1)} %bitcast.86), kind=kOutput, calls=%fused_computation.60 | convolution fusion | flops 415237632 | bytes 14426112 | tf_op jit(solution)/shard_map/while/body/eval_jaxpr/sub | solution.py:32
  181.7 7.0 %fusion.25 = bf16[512,4,64]{0,2,1:T(8,128)(2,1)S(1)} fusion(bf16[1536,4,64]{0,2,1:T(8,128)(2,1)} %bitcast.85, f32[4,512,1536]{2,1,0:T(8,128)} %get-tuple-element.93, f32[4,512]{1,0:T(4,128)S(1)} %get-tuple-element.92), kind=kOutput, calls=%fused_computation.45 | convolution fusion | flops 409075712 | bytes 13639680 | tf_op jit(solution)/shard_map/while/body/eval_jaxpr/hqk,khd->qhd/dot_general | solution.py:110
  189.6 3.4 %all-to-all-start = ((bf16[4,128,256]{1,2,0:T(8,128)(2,1)}), bf16[4,128,256]{1,2,0:T(8,128)(2,1)S(1)}, u32[]{:S(2)}, u32[]{:S(2)}) async-start(bf16[4,128,256]{1,2,0:T(8,128)(2,1)} %copy.18), calls=%async_computation | async-start | bytes 524288 | tf_op jit(solution)/shard_map/all_to_all | solution.py:118
  193.0 5.9 %all-to-all-done = bf16[4,128,256]{1,2,0:T(8,128)(2,1)S(1)} async-done(((bf16[4,128,256]{1,2,0:T(8,128)(2,1)}), bf16[4,128,256]{1,2,0:T(8,128)(2,1)S(1)}, u32[]{:S(2)}, u32[]{:S(2)}) %all-to-all-start) | async-done | bytes 262176 | tf_op jit(solution)/shard_map/all_to_all | solution.py:118
  199.0 2.8 %fusion.24 = bf16[128,1024]{1,0:T(8,128)(2,1)} fusion(bf16[128,1024]{0,1:T(8,128)(2,1)S(1)} %bitcast.82, bf16[1024,1024]{1,0:T(8,128)(2,1)} %all-gather.5.cloned.1.call-done, bf16[128,1024]{1,0:T(8,128)(2,1)S(1)} %copy-done.4), kind=kOutput, calls=%fused_computation.44 | convolution fusion | flops 268828672 | bytes 2883584 | tf_op jit(solution)/shard_map/dot_general | solution.py:120
  (58 shorter events, 17.0 us)
Async XLA Ops:
  6.5 27.1 %copy-start = (bf16[1024,1024]{1,0:T(8,128)(2,1)S(1)}, bf16[1024,1024]{1,0:T(8,128)(2,1)}, u32[]{:S(2)}) copy-start(bf16[1024,1024]{1,0:T(8,128)(2,1)} %param.13) | copy-start | bytes 6291460
  6.5 133.1 %all-gather.3.cloned.1.call-start = ((), (), s32[]{:S(2)}) async-start(), calls=%async_computation.1 | async-start | bytes 1310720 | tf_op jit(solution)/shard_map/all_gather | solution.py:81
  18.6 3.3 %copy-start.3 = (bf16[2048,2048]{1,0:T(8,128)(2,1)}, bf16[2048,2048]{1,0:T(8,128)(2,1)S(1)}, u32[]{:S(2)}) copy-start(bf16[2048,2048]{1,0:T(8,128)(2,1)S(1)} %convolution_convert_fusion) | copy-start | bytes 25165828
  21.9 11.7 %copy-start.6 = (s32[2,8]{1,0:T(2,128)S(1)}, s32[2,8]{1,0:T(2,128)}, u32[]{:S(2)}) copy-start(s32[2,8]{1,0:T(2,128)} %param.18) | copy-start | bytes 196
  21.9 11.7 %copy-start.5 = (bf16[128,1024]{1,0:T(8,128)(2,1)S(1)}, bf16[128,1024]{1,0:T(8,128)(2,1)}, u32[]{:S(2)}) copy-start(bf16[128,1024]{1,0:T(8,128)(2,1)} %param.12) | copy-start | bytes 786436
  26.1 16.3 %collective-permute-start.1 = (bf16[2,262144]{1,0:T(2,128)(2,1)}, bf16[2,262144]{1,0:T(2,128)(2,1)}, u32[]{:S(2)}, u32[]{:S(2)}) collective-permute-start(bf16[2,262144]{1,0:T(2,128)(2,1)} %slice.36), channel_id=1, source_target_pairs={{1,0},{2,1},{3,2},{4,3},{5,4},{6,5},{7,6},{8,7},{9,8},{10,9},{11,1... | collective-permute-start | bytes 3145736 | tf_op jit(solution)/shard_map/ppermute | solution.py:24
  31.5 18.3 %collective-permute-start = (bf16[2,262144]{1,0:T(2,128)(2,1)}, bf16[2,262144]{1,0:T(2,128)(2,1)}, u32[]{:S(2)}, u32[]{:S(2)}) collective-permute-start(bf16[2,262144]{1,0:T(2,128)(2,1)} %slice.34), channel_id=1, source_target_pairs={{0,1},{1,2},{2,3},{3,4},{4,5},{5,6},{6,7},{7,8},{8,9},{9,10},{10,1... | collective-permute-start | bytes 3145736 | tf_op jit(solution)/shard_map/ppermute | solution.py:23
  51.4 10.7 %copy-start.7 = (s32[2]{0:T(128)S(1)}, s32[2]{0:T(128)}, u32[]{:S(2)}) copy-start(s32[2]{0:T(128)} %param.19) | copy-start | bytes 28
  78.6 3.3 %copy-start.2 = (bf16[1024,1024]{1,0:T(8,128)(2,1)S(1)}, bf16[1024,1024]{1,0:T(8,128)(2,1)}, u32[]{:S(2)}) copy-start(bf16[1024,1024]{1,0:T(8,128)(2,1)} %get-tuple-element.135) | copy-start | bytes 6291460 | tf_op jit(solution)/shard_map/while
  104.9 3.3 %copy-start.2 = (bf16[1024,1024]{1,0:T(8,128)(2,1)S(1)}, bf16[1024,1024]{1,0:T(8,128)(2,1)}, u32[]{:S(2)}) copy-start(bf16[1024,1024]{1,0:T(8,128)(2,1)} %get-tuple-element.135) | copy-start | bytes 6291460 | tf_op jit(solution)/shard_map/while
  117.3 75.7 %all-gather.5.cloned.1.call-start = ((), (), s32[]{:S(2)}) async-start(), calls=%async_computation.2 | async-start | bytes 2621440 | tf_op jit(solution)/shard_map/all_gather | solution.py:119
  142.5 26.2 %collective-permute-start.2 = (bf16[512,512]{0,1:T(8,128)(2,1)S(1)}, bf16[512,512]{0,1:T(8,128)(2,1)S(1)}, u32[]{:S(2)}, u32[]{:S(2)}) collective-permute-start(bf16[512,512]{0,1:T(8,128)(2,1)S(1)} %slice.49), channel_id=1, source_target_pairs={{0,4},{4,8},{8,12},{12,16},{16,20},{20,24},{24,28},{1,5},{5,9},{9,... | collective-permute-start | bytes 1572872 | tf_op jit(solution)/shard_map/ppermute | solution.py:23
  145.9 24.7 %collective-permute-start.3 = (bf16[512,512]{0,1:T(8,128)(2,1)S(1)}, bf16[512,512]{0,1:T(8,128)(2,1)S(1)}, u32[]{:S(2)}, u32[]{:S(2)}) collective-permute-start(bf16[512,512]{0,1:T(8,128)(2,1)S(1)} %slice.49), channel_id=1, source_target_pairs={{4,0},{8,4},{12,8},{16,12},{20,16},{24,20},{28,24},{5,1},{9,5},{13... | collective-permute-start | bytes 1572872 | tf_op jit(solution)/shard_map/ppermute | solution.py:24
  181.7 17.3 %copy-start.4 = (bf16[128,1024]{1,0:T(8,128)(2,1)S(1)}, bf16[128,1024]{1,0:T(8,128)(2,1)}, u32[]{:S(2)}) copy-start(bf16[128,1024]{1,0:T(8,128)(2,1)} %fusion.23) | copy-start | bytes 786436
  181.7 20.0 %copy-start.1 = (bf16[1024,1024]{1,0:T(8,128)(2,1)S(1)}, bf16[1024,1024]{1,0:T(8,128)(2,1)}, u32[]{:S(2)}) copy-start(bf16[1024,1024]{1,0:T(8,128)(2,1)} %param.13) | copy-start | bytes 6291460
  189.6 9.4 %all-to-all-start = ((bf16[4,128,256]{1,2,0:T(8,128)(2,1)}), bf16[4,128,256]{1,2,0:T(8,128)(2,1)S(1)}, u32[]{:S(2)}, u32[]{:S(2)}) async-start(bf16[4,128,256]{1,2,0:T(8,128)(2,1)} %copy.18), calls=%async_computation | async-start | bytes 524288 | tf_op jit(solution)/shard_map/all_to_all | solution.py:118
Sparse Core Ops, SparseCore 0:
  117.4 22.1 all-gather.2
  141.2 22.5 all-gather.4
where the time goes:
time: 209 us
  waiting for transfers between devices  62.4 us (30%)
  local copies, waits for them, and re-layouts  50.2 us (24%)
  matrix products  46.2 us (22%)
  other arithmetic  19.7 us (9%)
  starting transfers between devices  16.2 us (8%)
  between operations  13.6 us (7%)
    ppermute x2, waiting for transfers between devices, extended(): before = lax.ppermute(last, axis, up)  24 us
    all_gather x1, waiting for transfers between devices, local(): piece = lax.all_gather(mesh_state, 'head', axis=0, tiled=True)  21.6 us
    gather x2, local copies, waits for them, and re-layouts, one_tile(): gathered = grid_tiles[tile_list].reshape(LIST * GT, 2 * model_width)  13.7 us
    dot_general x1, matrix products, local(): jnp.dot(grid_feat, enc_keyval, preferred_element_type=jnp.float32)  12.1 us
    while x8, local copies, waits for them, and re-layouts  10.9 us
    concatenate x2, other arithmetic, extended(): shard = jnp.concatenate([before, shard, after], axis=dim)  10.8 us
    ppermute x2, waiting for transfers between devices, extended(): after = lax.ppermute(first, axis, down)  10.2 us
    sub x1, matrix products, masked_softmax(): weights = jnp.exp(scores - row_top)  9.82 us
  transfers between devices with their start and end apart: 7, of which 6 were waited for; matrix products, arithmetic and copies ran while one was open for 13% of the time, Pallas kernels for 0%

commit v1 on v0

--- a/solution.py
+++ b/solution.py
@@ -78,7 +78,12 @@
         + jnp.dot(enc_attn, enc_out, preferred_element_type=jnp.float32)
     ).astype(jnp.bfloat16)
     head_cols = proc_qkv.shape[2]
-    piece = lax.all_gather(mesh_state, "head", axis=0, tiled=True)
+    ring = [mesh_state]
+    for hop in range(3):
+        ring.append(lax.ppermute(ring[-1], "head", [(dev, (dev + 1) % 4) for dev in range(4)]))
+    piece = jnp.roll(
+        jnp.concatenate(ring[::-1], axis=0), (lax.axis_index("head") + 1) * ring[0].shape[0], axis=0
+    )
     product = jnp.einsum("rd,tdc->rtc", piece, proc_qkv, preferred_element_type=jnp.float32)
     projected = product.astype(jnp.bfloat16).reshape(piece.shape[0], 3 * head_cols)
     group_rows = projected.shape[0]

time: 209 us -> 205 us (0.981)
  waiting for transfers between devices: 62.4 us -> 43.1 us
  blocking collectives: 0 us -> 8.39 us
  starting transfers between devices: 16.2 us -> 24.4 us
    all_gather x1 -> x0, waiting for transfers between devices: 21.6 us -> none  [local(): piece = lax.all_gather(mesh_state, 'head', axis=0, tiled=True)]
    ppermute x0 -> x3, starting transfers between devices: none -> 11 us  [local(): lax.ppermute(ring[-1], 'head', [(dev, (dev + 1) % 4) for dev in range(4)])]
    all_to_all x0 -> x1, blocking collectives: none -> 8.39 us  [local(): lax.all_to_all(proc_attn, 'head', split_axis=0, concat_axis=1, tiled=True)]
    ppermute x0 -> x3, waiting for transfers between devices: none -> 8.21 us  [local(): lax.ppermute(ring[-1], 'head', [(dev, (dev + 1) % 4) for dev in range(4)])]
    all_to_all x1 -> x0, waiting for transfers between devices: 5.94 us -> none  [local(): lax.all_to_all(proc_attn, 'head', split_axis=0, concat_axis=1, tiled=True)]
    all_to_all x1 -> x0, starting transfers between devices: 3.4 us -> none  [local(): lax.all_to_all(proc_attn, 'head', split_axis=0, concat_axis=1, tiled=True)]
    unnamed x16 -> x21, local copies, waits for them, and re-layouts: 6.48 us -> 6.62 us
  transfers between devices with their start and end apart: 7 -> 8, of which waited for: 6 -> 7; matrix products, arithmetic and copies ran while one was open for 13% -> 13% of each run, Pallas kernels for 0% -> 0%
where the time goes in v1:
time: 205 us; the launch traced here: 204 us
  local copies, waits for them, and re-layouts  49.7 us (24%)
  matrix products  45.2 us (22%)
  waiting for transfers between devices  43.1 us (21%)
  starting transfers between devices  24.4 us (12%)
  other arithmetic  19.5 us (10%)
  between operations  13.7 us (7%)
  blocking collectives  8.39 us (4%)
    ppermute x2, waiting for transfers between devices, extended(): before = lax.ppermute(last, axis, up)  25.1 us
    gather x2, local copies, waits for them, and re-layouts, one_tile(): gathered = grid_tiles[tile_list].reshape(LIST * GT, 2 * model_width)  13.7 us
    dot_general x1, matrix products, local(): jnp.dot(grid_feat, enc_keyval, preferred_element_type=jnp.float32)  12.1 us
    ppermute x3, starting transfers between devices, local(): lax.ppermute(ring[-1], 'head', [(dev, (dev + 1) % 4) for dev in range(4)])  11 us
    while x8, local copies, waits for them, and re-layouts  10.8 us
    concatenate x2, other arithmetic, extended(): shard = jnp.concatenate([before, shard, after], axis=dim)  10.8 us
    sub x1, matrix products, masked_softmax(): weights = jnp.exp(scores - row_top)  9.82 us
    ppermute x2, waiting for transfers between devices, extended(): after = lax.ppermute(first, axis, down)  9.75 us
  transfers between devices with their start and end apart: 8, of which 7 were waited for; matrix products, arithmetic and copies ran while one was open for 13% of the time, Pallas kernels for 0%

profile of v1, /device:TPU:8, one launch (start us, length us, event | category | flops | bytes accessed | tf_op | source)
XLA Modules:
  0.0 204.1 jit_solution(6309490997285459647)
XLA Ops:
  6.5 12.1 %convolution_convert_fusion = bf16[2048,2048]{1,0:T(8,128)(2,1)S(1)} fusion(bf16[2048,1024]{1,0:T(8,128)(2,1)} %param.11, bf16[1024,2048]{1,0:T(8,128)(2,1)} %param.14), kind=kOutput, calls=%fused_computation.30 | convolution fusion | flops 8594128896 | bytes 16777216 | tf_op jit(solution)/shard_map/dot_general | solution.py:45
  18.6 3.3 %copy-done.3 = bf16[2048,2048]{1,0:T(8,128)(2,1)} copy-done((bf16[2048,2048]{1,0:T(8,128)(2,1)}, bf16[2048,2048]{1,0:T(8,128)(2,1)S(1)}, u32[]{:S(2)}) %copy-start.3) | copy-done | bytes 8388632
  23.1 3.0 %slice.36 = bf16[2,262144]{1,0:T(2,128)(2,1)} reshape(bf16[256,2048]{1,0:T(8,128)(2,1)} %get-tuple-element.89) | data formatting | bytes 2097152 | tf_op jit(solution)/shard_map/slice | solution.py:22
  26.2 3.7 %collective-permute-start.1 = (bf16[2,262144]{1,0:T(2,128)(2,1)}, bf16[2,262144]{1,0:T(2,128)(2,1)}, u32[]{:S(2)}, u32[]{:S(2)}) collective-permute-start(bf16[2,262144]{1,0:T(2,128)(2,1)} %slice.36), channel_id=1, source_target_pairs={{1,0},{2,1},{3,2},{4,3},{5,4},{6,5},{7,6},{8,7},{9,8},{10,9},{11,1... | collective-permute-start | bytes 3145736 | tf_op jit(solution)/shard_map/ppermute | solution.py:24
  34.2 8.3 %collective-permute-done.1 = bf16[2,262144]{1,0:T(2,128)(2,1)} collective-permute-done((bf16[2,262144]{1,0:T(2,128)(2,1)}, bf16[2,262144]{1,0:T(2,128)(2,1)}, u32[]{:S(2)}, u32[]{:S(2)}) %collective-permute-start.1) | collective-permute-done | bytes 1048608 | tf_op jit(solution)/shard_map/ppermute | solution.py:24
  44.1 5.8 %collective-permute-done = bf16[2,262144]{1,0:T(2,128)(2,1)} collective-permute-done((bf16[2,262144]{1,0:T(2,128)(2,1)}, bf16[2,262144]{1,0:T(2,128)(2,1)}, u32[]{:S(2)}, u32[]{:S(2)}) %collective-permute-start) | collective-permute-done | bytes 1048608 | tf_op jit(solution)/shard_map/ppermute | solution.py:23
  51.5 10.7 %pad_maximum_fusion = bf16[20,128,2048]{2,1,0:T(8,128)(2,1)} fusion(bf16[2,128,2048]{2,1,0:T(8,128)(2,1)S(1)} %bitcast.79, bf16[16,128,2048]{2,1,0:T(8,128)(2,1)} %bitcast.77, bf16[2,128,2048]{2,1,0:T(8,128)(2,1)S(1)} %bitcast.80), kind=kLoop, calls=%fused_computation.28 | loop fusion | flops 10485760 | bytes 20971520 | tf_op jit(solution)/shard_map/concatenate | solution.py:25
  62.2 52.1 %while.3 = (s32[]{:T(128)}, bf16[2,64,1024]{2,1,0:T(8,128)(2,1)S(1)}, s32[2,8]{1,0:T(2,128)S(1)}, bf16[20,128,2048]{2,1,0:T(8,128)(2,1)}, s32[2]{0:T(128)S(1)}, /*index=5*/bf16[2,64,1024]{2,1,0:T(8,128)(2,1)S(1)}, s32[]{:T(128)}) while((s32[]{:T(128)}, bf16[2,64,1024]{2,1,0:T(8,128)(2,1)S(1)}, s32[2,8]{1,0:T(2,128)S(1)}, ...), condition=%wide.region_3.4_spmd.clone, body=%wide.region_0.3_spmd.clone.sunk | while | flops 276892704 | bytes 55851268 | solution.py:72
  62.2 6.8 %gather_fusion = bf16[8,128,2048]{2,1,0:T(8,128)(2,1)} fusion(bf16[20,128,2048]{2,1,0:T(8,128)(2,1)} %get-tuple-element.156, s32[1024]{0:T(1024)S(1)} %pad_clamp_fusion.2), kind=kCustom, calls=%fused_computation.clone.clone.1 | custom fusion | bytes 8388640 | tf_op jit(solution)/shard_map/while/body/eval_jaxpr/gather | solution.py:58
  69.1 4.7 %fusion.66 = (bf16[1024,1024]{1,0:T(8,128)(2,1)}, bf16[1024,1024]{1,0:T(8,128)(2,1)}) fusion(bf16[1024,2048]{1,0:T(8,128)(2,1)} %bitcast.74), kind=kLoop, calls=%fused_computation.66.clone.1 | loop fusion | bytes 8388608 | tf_op jit(solution)/shard_map/while/body/eval_jaxpr/slice | solution.py:59
  73.7 2.9 %copy.38 = bf16[1024,1024]{0,1:T(8,128)(2,1)S(1)} copy(bf16[1024,1024]{1,0:T(8,128)(2,1)} %get-tuple-element.136) | data formatting | bytes 4194304 | tf_op jit(solution)/shard_map/while
  78.6 3.3 %fusion.68 = (f32[16,64]{1,0:T(8,128)S(1)}, f32[16,64,1024]{2,1,0:T(8,128)}) fusion(f32[16,64,1024]{2,1,0:T(8,128)S(1)} %fusion.67, pred[1024]{0:T(1024)(128)(4,1)S(1)} %iota_compare_fusion.2), kind=kOutput, calls=%fused_computation.67.clone.1 | output fusion | flops 6292479 | bytes 8393728 | tf_op jit(solution)/shard_map/while/body/eval_jaxpr/sub | solution.py:32
  81.9 2.6 %copy.37 = bf16[1024,1024]{0,1:T(8,128)(2,1)} copy(bf16[1024,1024]{1,0:T(8,128)(2,1)S(1)} %copy-done.2) | data formatting | bytes 4194304 | tf_op jit(solution)/shard_map/while
  84.5 3.6 %fusion.69 = bf16[16,64,64]{2,1,0:T(8,128)(2,1)S(1)} fusion(bf16[1024,16,64]{0,2,1:T(8,128)(2,1)} %bitcast.76, f32[16,64,1024]{2,1,0:T(8,128)} %get-tuple-element.137, f32[16,64]{1,0:T(8,128)S(1)} %get-tuple-element.138), kind=kOutput, calls=%fused_computation.11.clone.1 | convolution fusion | flops 136380416 | bytes 6426624 | tf_op jit(solution)/shard_map/while/body/eval_jaxpr/hqk,khd->qhd/dot_general | solution.py:67
  88.3 6.8 %gather_fusion = bf16[8,128,2048]{2,1,0:T(8,128)(2,1)} fusion(bf16[20,128,2048]{2,1,0:T(8,128)(2,1)} %get-tuple-element.156, s32[1024]{0:T(1024)S(1)} %pad_clamp_fusion.2), kind=kCustom, calls=%fused_computation.clone.clone.1 | custom fusion | bytes 8388640 | tf_op jit(solution)/shard_map/while/body/eval_jaxpr/gather | solution.py:58
  95.1 4.7 %fusion.66 = (bf16[1024,1024]{1,0:T(8,128)(2,1)}, bf16[1024,1024]{1,0:T(8,128)(2,1)}) fusion(bf16[1024,2048]{1,0:T(8,128)(2,1)} %bitcast.74), kind=kLoop, calls=%fused_computation.66.clone.1 | loop fusion | bytes 8388608 | tf_op jit(solution)/shard_map/while/body/eval_jaxpr/slice | solution.py:59
  99.8 2.9 %copy.38 = bf16[1024,1024]{0,1:T(8,128)(2,1)S(1)} copy(bf16[1024,1024]{1,0:T(8,128)(2,1)} %get-tuple-element.136) | data formatting | bytes 4194304 | tf_op jit(solution)/shard_map/while
  104.7 3.3 %fusion.68 = (f32[16,64]{1,0:T(8,128)S(1)}, f32[16,64,1024]{2,1,0:T(8,128)}) fusion(f32[16,64,1024]{2,1,0:T(8,128)S(1)} %fusion.67, pred[1024]{0:T(1024)(128)(4,1)S(1)} %iota_compare_fusion.2), kind=kOutput, calls=%fused_computation.67.clone.1 | output fusion | flops 6292479 | bytes 8393728 | tf_op jit(solution)/shard_map/while/body/eval_jaxpr/sub | solution.py:32
  108.0 2.6 %copy.37 = bf16[1024,1024]{0,1:T(8,128)(2,1)} copy(bf16[1024,1024]{1,0:T(8,128)(2,1)S(1)} %copy-done.2) | data formatting | bytes 4194304 | tf_op jit(solution)/shard_map/while
  110.5 3.6 %fusion.69 = bf16[16,64,64]{2,1,0:T(8,128)(2,1)S(1)} fusion(bf16[1024,16,64]{0,2,1:T(8,128)(2,1)} %bitcast.76, f32[16,64,1024]{2,1,0:T(8,128)} %get-tuple-element.137, f32[16,64]{1,0:T(8,128)S(1)} %get-tuple-element.138), kind=kOutput, calls=%fused_computation.11.clone.1 | convolution fusion | flops 136380416 | bytes 6426624 | tf_op jit(solution)/shard_map/while/body/eval_jaxpr/hqk,khd->qhd/dot_general | solution.py:67
  116.4 4.9 %collective-permute-start.2 = (bf16[128,1024]{1,0:T(8,128)(2,1)S(1)}, bf16[128,1024]{1,0:T(8,128)(2,1)S(1)}, u32[]{:S(2)}, u32[]{:S(2)}) collective-permute-start(bf16[128,1024]{1,0:T(8,128)(2,1)S(1)} %fusion.23), channel_id=1, source_target_pairs={{0,1},{1,2},{2,3},{3,0},{4,5},{5,6},{6,7},{7,4},{8,9},{9,10},{10,1... | collective-permute-start | bytes 786440 | tf_op jit(solution)/shard_map/ppermute | solution.py:83
  121.3 2.8 %collective-permute-done.2 = bf16[128,1024]{1,0:T(8,128)(2,1)S(1)} collective-permute-done((bf16[128,1024]{1,0:T(8,128)(2,1)S(1)}, bf16[128,1024]{1,0:T(8,128)(2,1)S(1)}, u32[]{:S(2)}, u32[]{:S(2)}) %collective-permute-start.2) | collective-permute-done | bytes 262176 | tf_op jit(solution)/shard_map/ppermute | solution.py:83
  124.1 3.0 %collective-permute-start.3 = (bf16[128,1024]{1,0:T(8,128)(2,1)S(1)}, bf16[128,1024]{1,0:T(8,128)(2,1)S(1)}, u32[]{:S(2)}, u32[]{:S(2)}) collective-permute-start(bf16[128,1024]{1,0:T(8,128)(2,1)S(1)} %collective-permute-done.2), channel_id=1, source_target_pairs={{0,1},{1,2},{2,3},{3,0},{4,5},{5,6},{6,7},{7,4},{8,9},{9,10},{10,1... | collective-permute-start | bytes 786440 | tf_op jit(solution)/shard_map/ppermute | solution.py:83
  127.1 2.8 %collective-permute-done.3 = bf16[128,1024]{1,0:T(8,128)(2,1)S(1)} collective-permute-done((bf16[128,1024]{1,0:T(8,128)(2,1)S(1)}, bf16[128,1024]{1,0:T(8,128)(2,1)S(1)}, u32[]{:S(2)}, u32[]{:S(2)}) %collective-permute-start.3) | collective-permute-done | bytes 262176 | tf_op jit(solution)/shard_map/ppermute | solution.py:83
  129.9 3.0 %collective-permute-start.4 = (bf16[128,1024]{1,0:T(8,128)(2,1)S(1)}, bf16[128,1024]{1,0:T(8,128)(2,1)S(1)}, u32[]{:S(2)}, u32[]{:S(2)}) collective-permute-start(bf16[128,1024]{1,0:T(8,128)(2,1)S(1)} %collective-permute-done.3), channel_id=1, source_target_pairs={{0,1},{1,2},{2,3},{3,0},{4,5},{5,6},{6,7},{7,4},{8,9},{9,10},{10,1... | collective-permute-start | bytes 786440 | tf_op jit(solution)/shard_map/ppermute | solution.py:83
  133.0 2.7 %collective-permute-done.4 = bf16[128,1024]{1,0:T(8,128)(2,1)S(1)} collective-permute-done((bf16[128,1024]{1,0:T(8,128)(2,1)S(1)}, bf16[128,1024]{1,0:T(8,128)(2,1)S(1)}, u32[]{:S(2)}, u32[]{:S(2)}) %collective-permute-start.4) | collective-permute-done | bytes 262176 | tf_op jit(solution)/shard_map/ppermute | solution.py:83
  138.4 5.5 %collective-permute-start.5 = (bf16[512,512]{0,1:T(8,128)(2,1)S(1)}, bf16[512,512]{0,1:T(8,128)(2,1)S(1)}, u32[]{:S(2)}, u32[]{:S(2)}) collective-permute-start(bf16[512,512]{0,1:T(8,128)(2,1)S(1)} %slice.49), channel_id=1, source_target_pairs={{0,4},{4,8},{8,12},{12,16},{16,20},{20,24},{24,28},{1,5},{5,9},{9,... | collective-permute-start | bytes 1572872 | tf_op jit(solution)/shard_map/ppermute | solution.py:23
  147.0 19.2 %collective-permute-done.5 = bf16[512,512]{0,1:T(8,128)(2,1)S(1)} collective-permute-done((bf16[512,512]{0,1:T(8,128)(2,1)S(1)}, bf16[512,512]{0,1:T(8,128)(2,1)S(1)}, u32[]{:S(2)}, u32[]{:S(2)}) %collective-permute-start.5) | collective-permute-done | bytes 524320 | tf_op jit(solution)/shard_map/ppermute | solution.py:23
  169.1 9.8 %fusion.37 = (f32[4,512]{1,0:T(4,128)S(1)}, f32[4,512,1536]{2,1,0:T(8,128)}) fusion(pred[512,1536]{1,0:T(8,128)(4,1)S(1)} %fusion.21, bf16[512,4,64]{0,2,1:T(8,128)(2,1)S(1)} %bitcast.87, bf16[1536,4,64]{0,2,1:T(8,128)(2,1)} %bitcast.86), kind=kOutput, calls=%fused_computation.70 | convolution fusion | flops 415237632 | bytes 14426112 | tf_op jit(solution)/shard_map/while/body/eval_jaxpr/sub | solution.py:32
  178.9 7.0 %fusion.25 = bf16[512,4,64]{0,2,1:T(8,128)(2,1)S(1)} fusion(bf16[1536,4,64]{0,2,1:T(8,128)(2,1)} %bitcast.85, f32[4,512,1536]{2,1,0:T(8,128)} %get-tuple-element.93, f32[4,512]{1,0:T(4,128)S(1)} %get-tuple-element.92), kind=kOutput, calls=%fused_computation.45 | convolution fusion | flops 409075712 | bytes 13639680 | tf_op jit(solution)/shard_map/while/body/eval_jaxpr/hqk,khd->qhd/dot_general | solution.py:115
  186.1 8.4 %all_to_all.16 = bf16[4,128,256]{1,2,0:T(8,128)(2,1)S(1)} all-to-all(bf16[4,128,256]{1,2,0:T(8,128)(2,1)S(1)} %copy.18), channel_id=1, replica_groups=mesh['band'=8,'head'=4] {'head'}, dimensions={0} | all-to-all | bytes 524288 | tf_op jit(solution)/shard_map/all_to_all | solution.py:123
  194.5 2.8 %fusion.24 = bf16[128,1024]{1,0:T(8,128)(2,1)} fusion(bf16[128,1024]{0,1:T(8,128)(2,1)S(1)} %bitcast.82, bf16[1024,1024]{1,0:T(8,128)(2,1)} %all-gather.2.cloned.1.call-done, bf16[128,1024]{1,0:T(8,128)(2,1)S(1)} %fusion.23), kind=kOutput, calls=%fused_computation.44 | convolution fusion | flops 268828672 | bytes 2883584 | tf_op jit(solution)/shard_map/dot_general | solution.py:125
  (66 shorter events, 23.8 us)
Async XLA Ops:
  6.5 27.2 %copy-start = (bf16[1024,1024]{1,0:T(8,128)(2,1)S(1)}, bf16[1024,1024]{1,0:T(8,128)(2,1)}, u32[]{:S(2)}) copy-start(bf16[1024,1024]{1,0:T(8,128)(2,1)} %param.13) | copy-start | bytes 6291460
  6.5 188.0 %all-gather.2.cloned.1.call-start = ((), (), s32[]{:S(2)}) async-start(), calls=%async_computation.1 | async-start | bytes 2621440 | tf_op jit(solution)/shard_map/all_gather | solution.py:124
  18.6 3.3 %copy-start.3 = (bf16[2048,2048]{1,0:T(8,128)(2,1)}, bf16[2048,2048]{1,0:T(8,128)(2,1)S(1)}, u32[]{:S(2)}) copy-start(bf16[2048,2048]{1,0:T(8,128)(2,1)S(1)} %convolution_convert_fusion) | copy-start | bytes 25165828
  23.1 10.6 %copy-start.5 = (s32[2,8]{1,0:T(2,128)S(1)}, s32[2,8]{1,0:T(2,128)}, u32[]{:S(2)}) copy-start(s32[2,8]{1,0:T(2,128)} %param.18) | copy-start | bytes 196
  23.1 10.6 %copy-start.4 = (bf16[128,1024]{1,0:T(8,128)(2,1)S(1)}, bf16[128,1024]{1,0:T(8,128)(2,1)}, u32[]{:S(2)}) copy-start(bf16[128,1024]{1,0:T(8,128)(2,1)} %param.12) | copy-start | bytes 786436
  26.2 16.3 %collective-permute-start.1 = (bf16[2,262144]{1,0:T(2,128)(2,1)}, bf16[2,262144]{1,0:T(2,128)(2,1)}, u32[]{:S(2)}, u32[]{:S(2)}) collective-permute-start(bf16[2,262144]{1,0:T(2,128)(2,1)} %slice.36), channel_id=1, source_target_pairs={{1,0},{2,1},{3,2},{4,3},{5,4},{6,5},{7,6},{8,7},{9,8},{10,9},{11,1... | collective-permute-start | bytes 3145736 | tf_op jit(solution)/shard_map/ppermute | solution.py:24
  31.6 18.3 %collective-permute-start = (bf16[2,262144]{1,0:T(2,128)(2,1)}, bf16[2,262144]{1,0:T(2,128)(2,1)}, u32[]{:S(2)}, u32[]{:S(2)}) collective-permute-start(bf16[2,262144]{1,0:T(2,128)(2,1)} %slice.34), channel_id=1, source_target_pairs={{0,1},{1,2},{2,3},{3,4},{4,5},{5,6},{6,7},{7,8},{8,9},{9,10},{10,1... | collective-permute-start | bytes 3145736 | tf_op jit(solution)/shard_map/ppermute | solution.py:23
  51.5 10.7 %copy-start.6 = (s32[2]{0:T(128)S(1)}, s32[2]{0:T(128)}, u32[]{:S(2)}) copy-start(s32[2]{0:T(128)} %param.19) | copy-start | bytes 28
  78.6 3.3 %copy-start.2 = (bf16[1024,1024]{1,0:T(8,128)(2,1)S(1)}, bf16[1024,1024]{1,0:T(8,128)(2,1)}, u32[]{:S(2)}) copy-start(bf16[1024,1024]{1,0:T(8,128)(2,1)} %get-tuple-element.135) | copy-start | bytes 6291460 | tf_op jit(solution)/shard_map/while
  104.7 3.3 %copy-start.2 = (bf16[1024,1024]{1,0:T(8,128)(2,1)S(1)}, bf16[1024,1024]{1,0:T(8,128)(2,1)}, u32[]{:S(2)}) copy-start(bf16[1024,1024]{1,0:T(8,128)(2,1)} %get-tuple-element.135) | copy-start | bytes 6291460 | tf_op jit(solution)/shard_map/while
  116.4 7.7 %collective-permute-start.2 = (bf16[128,1024]{1,0:T(8,128)(2,1)S(1)}, bf16[128,1024]{1,0:T(8,128)(2,1)S(1)}, u32[]{:S(2)}, u32[]{:S(2)}) collective-permute-start(bf16[128,1024]{1,0:T(8,128)(2,1)S(1)} %fusion.23), channel_id=1, source_target_pairs={{0,1},{1,2},{2,3},{3,0},{4,5},{5,6},{6,7},{7,4},{8,9},{9,10},{10,1... | collective-permute-start | bytes 786440 | tf_op jit(solution)/shard_map/ppermute | solution.py:83
  124.1 5.8 %collective-permute-start.3 = (bf16[128,1024]{1,0:T(8,128)(2,1)S(1)}, bf16[128,1024]{1,0:T(8,128)(2,1)S(1)}, u32[]{:S(2)}, u32[]{:S(2)}) collective-permute-start(bf16[128,1024]{1,0:T(8,128)(2,1)S(1)} %collective-permute-done.2), channel_id=1, source_target_pairs={{0,1},{1,2},{2,3},{3,0},{4,5},{5,6},{6,7},{7,4},{8,9},{9,10},{10,1... | collective-permute-start | bytes 786440 | tf_op jit(solution)/shard_map/ppermute | solution.py:83
  129.9 5.8 %collective-permute-start.4 = (bf16[128,1024]{1,0:T(8,128)(2,1)S(1)}, bf16[128,1024]{1,0:T(8,128)(2,1)S(1)}, u32[]{:S(2)}, u32[]{:S(2)}) collective-permute-start(bf16[128,1024]{1,0:T(8,128)(2,1)S(1)} %collective-permute-done.3), channel_id=1, source_target_pairs={{0,1},{1,2},{2,3},{3,0},{4,5},{5,6},{6,7},{7,4},{8,9},{9,10},{10,1... | collective-permute-start | bytes 786440 | tf_op jit(solution)/shard_map/ppermute | solution.py:83
  138.4 27.9 %collective-permute-start.5 = (bf16[512,512]{0,1:T(8,128)(2,1)S(1)}, bf16[512,512]{0,1:T(8,128)(2,1)S(1)}, u32[]{:S(2)}, u32[]{:S(2)}) collective-permute-start(bf16[512,512]{0,1:T(8,128)(2,1)S(1)} %slice.49), channel_id=1, source_target_pairs={{0,4},{4,8},{8,12},{12,16},{16,20},{20,24},{24,28},{1,5},{5,9},{9,... | collective-permute-start | bytes 1572872 | tf_op jit(solution)/shard_map/ppermute | solution.py:23
  143.8 23.9 %collective-permute-start.6 = (bf16[512,512]{0,1:T(8,128)(2,1)S(1)}, bf16[512,512]{0,1:T(8,128)(2,1)S(1)}, u32[]{:S(2)}, u32[]{:S(2)}) collective-permute-start(bf16[512,512]{0,1:T(8,128)(2,1)S(1)} %slice.49), channel_id=1, source_target_pairs={{4,0},{8,4},{12,8},{16,12},{20,16},{24,20},{28,24},{5,1},{9,5},{13... | collective-permute-start | bytes 1572872 | tf_op jit(solution)/shard_map/ppermute | solution.py:24
  178.9 18.3 %copy-start.1 = (bf16[1024,1024]{1,0:T(8,128)(2,1)S(1)}, bf16[1024,1024]{1,0:T(8,128)(2,1)}, u32[]{:S(2)}) copy-start(bf16[1024,1024]{1,0:T(8,128)(2,1)} %param.13) | copy-start | bytes 6291460
Sparse Core Ops, SparseCore 0:
  133.0 23.1 all-gather.1
